TPU v7x, 32 devices: a whole 2x2x4 slice. The times are simulated.
32 devices in a mesh: row: 4 (over z), col: 8 (over y, x, core).
Axes of the slice: x: 2, y: 2, z: 4, core: 2. Of those that a mesh axis runs over, the one named last changes fastest.
Arguments:
- ancestor_pivot: float32 [8, 512, 4, 1024], P(None, 'row', None, 'col'), as said below
- child_pivot: float32 [8, 512, 4, 1024], P(None, 'row', None, 'col'), as said below
- child_panel: float32 [8, 512, 4, 1024], P(None, 'row', None, 'col'), may hold values from -0.09375 to 0.09375
- block_pattern: int32 [32, 32], replicated, may hold values 0 or 1
Outputs:
- child_inverse: float32 [8, 512, 4, 1024], P(None, 'row', None, 'col')
Inputs may be any that keep to these rules, and one draw needn't show every extreme that they name: ancestor_pivot is an exactly symmetric 4096 x 4096 matrix. child_pivot is an exactly symmetric 4096 x 4096 matrix.
All inputs are finite; a program needn't handle non-finite values.
Results may differ from a plain program's by a relative error of at most 0.00005.
Values sent between devices are 32-bit elements; how exact they have to be, the bound alone decides.
A program may use at most 128 MiB of HBM per device.

v0:
```python
import jax
import jax.numpy as jnp
from jax import lax
from jax.sharding import PartitionSpec as P


def column_term(stationary, local_rows, piece):
    shaped = piece.reshape(local_rows, piece.shape[2], piece.shape[3])
    return jnp.einsum(
        "kcl,kn->cln",
        shaped,
        stationary,
        precision=lax.Precision.HIGHEST,
        preferred_element_type=jnp.float32,
    )


def local(ancestor_pivot, child_pivot, child_panel, block_pattern):
    anc_blocks = child_panel.shape[0]
    block_size = child_panel.shape[1]
    col_blocks = child_panel.shape[2]
    anc_col_blocks = ancestor_pivot.shape[2]
    child_rows = child_pivot.shape[0]
    row_count = lax.axis_size("row")
    col_count = lax.axis_size("col")
    row_index = lax.axis_index("row")
    col_index = lax.axis_index("col")
    local_rows = anc_blocks * block_size
    local_cols = col_blocks * block_size
    blocks = block_pattern.reshape(anc_blocks, row_count, col_blocks, col_count)
    local_mask = lax.dynamic_index_in_dim(blocks, row_index, 1, keepdims=False)
    local_mask = lax.dynamic_index_in_dim(local_mask, col_index, 2, keepdims=False)
    masked = child_panel * local_mask.astype(jnp.float32)[:, None, :, None]
    masked_flat = masked.reshape(local_rows, local_cols)
    panel_all = lax.all_gather(masked, "row", axis=1, tiled=True)
    panel_split = panel_all.reshape(anc_col_blocks, col_count * block_size, local_cols)
    segment = lax.all_gather(ancestor_pivot, "col", axis=3, tiled=True)
    length = segment.shape[3]
    weights = segment.reshape(local_rows, anc_col_blocks, length)
    product = jnp.einsum(
        "kcl,cln->kn",
        weights,
        panel_split,
        precision=lax.Precision.HIGHEST,
        preferred_element_type=jnp.float32,
    )
    product_blocks = product.reshape(anc_blocks, block_size, col_blocks, block_size)
    term = column_term(
        masked_flat, local_rows, lax.all_gather(product_blocks, "col", axis=3, tiled=True)
    )
    term = term.reshape(child_rows, row_count, block_size, local_cols)
    term = jnp.transpose(term, (1, 0, 2, 3)).reshape(
        row_count * child_rows * block_size, local_cols
    )
    summed = lax.psum_scatter(term, "row", scatter_dimension=0, tiled=True)
    return child_pivot + summed.reshape(child_rows, block_size, col_blocks, block_size)


def solution(mesh):
    return jax.shard_map(
        local,
        mesh=mesh,
        in_specs=(
            P(None, "row", None, "col"),
            P(None, "row", None, "col"),
            P(None, "row", None, "col"),
            P(),
        ),
        out_specs=P(None, "row", None, "col"),
        check_vma=False,
    )
```

profile of v0, /device:TPU:0, one launch (start us, length us, event | category | flops | bytes accessed | tf_op | source)
XLA Modules:
  0.0 626.5 jit_solution(12353932388971323393)
XLA Ops:
  6.5 0.0 all-gather.4.cloned.1.call-start
  6.5 0.8 reshape.28
  7.4 0.1 constant_dynamic-slice_fusion
  7.4 0.1 copy.15
  7.6 0.1 copy.9
  7.6 3.4 broadcast_multiply_fusion
  11.0 0.0 all-gather.4.cloned.1.call-update
  11.0 0.0 all-gather.6.cloned.1.call-start
  11.1 0.7 all-gather.6.cloned.1.call-update
  11.8 0.0 all-gather.8.cloned.1.call-start
  11.8 151.7 %all-gather.4.cloned.1.call-done = f32[8,512,4,128]{3,2,1,0:T(4,128)} async-done(((f32[8,128,4,128]{3,2,1,0:T(4,128)}), f32[8,512,4,128]{3,2,1,0:T(4,128)}) %all-gather.4.cloned.1.call-update) | async-done | bytes 8388624 | tf_op jit(solution)/shard_map/all_gather | solution.py:35
  163.5 10.5 %reshape.29 = f32[4,1024,512]{2,1,0:T(8,128)} reshape(f32[8,512,4,128]{3,2,1,0:T(4,128)} %all-gather.4.cloned.1.call-done) | data formatting | bytes 16777216 | tf_op jit(solution)/shard_map/reshape | solution.py:36
  174.0 82.6 %all-gather.6.cloned.1.call-done = f32[8,128,4,1024]{3,2,1,0:T(4,128)} async-done(((f32[8,128,4,128]{3,2,1,0:T(4,128)}), f32[8,128,4,1024]{3,2,1,0:T(4,128)}) %all-gather.6.cloned.1.call-update) | async-done | bytes 16777232 | tf_op jit(solution)/shard_map/all_gather | solution.py:37
  256.6 0.0 copy-start.1
  256.6 15.3 %copy.10 = f32[8,128,4,1024]{3,1,0,2:T(8,128)S(1)} copy(f32[8,128,4,1024]{3,2,1,0:T(4,128)} %all-gather.6.cloned.1.call-done) | data formatting | bytes 33554432 | tf_op jit(solution)/shard_map/all_gather | solution.py:37
  272.0 0.0 copy-done.1
  272.0 0.0 copy-start
  272.0 54.8 %convolution_bitcast_fusion.1 = f32[64,8,8,128]{3,1,2,0:T(8,128)S(1)} fusion(f32[4,1024,512]{2,1,0:T(8,128)S(1)} %copy-done.1, f32[1024,4,1024]{2,0,1:T(8,128)S(1)} %bitcast.29), kind=kOutput, calls=%fused_computation.2 | convolution fusion | flops 25769803776 | bytes 27262976 | tf_op jit(solution)/shard_map/kcl,cln->kn/dot_general | solution.py:40
  326.9 1.8 copy.16
  328.6 0.0 all-gather.8.cloned.1.call-update
  328.7 0.0 reduce-scatter.2.cloned.1.call-start
  328.7 0.0 copy-done
  328.7 1.8 reshape.37
  330.6 0.0 copy-start.2
  330.6 88.0 %all-gather.8.cloned.1.call-done = f32[8,128,4,1024]{1,0,3,2:T(8,128)} async-done(((f32[8,128,4,128]{1,0,3,2:T(8,128)}), f32[8,128,4,1024]{1,0,3,2:T(8,128)}) %all-gather.8.cloned.1.call-update) | async-done | bytes 16777232 | tf_op jit(solution)/shard_map/all_gather | solution.py:49
  418.5 18.0 %reshape.32 = f32[1024,4,1024]{0,2,1:T(8,128)} reshape(f32[8,128,4,1024]{1,0,3,2:T(8,128)} %all-gather.8.cloned.1.call-done) | data formatting | bytes 33554432 | tf_op jit(solution)/shard_map/reshape | solution.py:8
  436.5 0.0 copy-done.2
  436.5 29.1 %convolution_bitcast_fusion = f32[4,8,128,512]{3,2,0,1:T(8,128)S(1)} fusion(f32[8,4,128,1024]{3,2,1,0:T(8,128)} %bitcast.30, f32[1024,512,1,1]{1,0,2,3:T(8,128)S(1)} %copy-done.2), kind=kOutput, calls=%fused_computation | convolution fusion | flops 25769803776 | bytes 27262976 | tf_op jit(solution)/shard_map/kcl,kn->cln/dot_general | solution.py:9
  465.6 4.2 copy.12
  469.8 0.0 reduce-scatter.2.cloned.1.call-update
  469.9 144.8 %reduce-scatter.2.cloned.1.call-done = f32[1024,512]{1,0:T(8,128)} async-done(((f32[4096,512]{1,0:T(8,128)}), f32[1024,512]{1,0:T(8,128)}) %reduce-scatter.2.cloned.1.call-update) | async-done | bytes 2097168 | tf_op jit(solution)/shard_map/reduce_scatter | solution.py:55
  614.6 1.9 reshape.35
  616.6 3.5 add.19
  (1 shorter events, 0.0 us)
Async XLA Ops:
  6.5 157.0 %all-gather.4.cloned.1.call-start = ((), (), s32[]{:S(2)}) async-start(), calls=%async_computation.1 | async-start | bytes 10485760 | tf_op jit(solution)/shard_map/all_gather | solution.py:35
  11.0 245.6 %all-gather.6.cloned.1.call-start = ((), (), s32[]{:S(2)}) async-start(), calls=%async_computation.2 | async-start | bytes 18874368 | tf_op jit(solution)/shard_map/all_gather | solution.py:37
  11.8 406.8 %all-gather.8.cloned.1.call-start = ((), (), s32[]{:S(2)}) async-start(), calls=%async_computation.3 | async-start | bytes 18874368 | tf_op jit(solution)/shard_map/all_gather | solution.py:49
  256.6 15.4 %copy-start.1 = (f32[4,1024,512]{2,1,0:T(8,128)S(1)}, f32[4,1024,512]{2,1,0:T(8,128)}, u32[]{:S(2)}) copy-start(f32[4,1024,512]{2,1,0:T(8,128)} %reshape.29) | copy-start | bytes 25165828
  272.0 56.7 %copy-start = (f32[8,128,4,128]{3,2,1,0:T(4,128)S(1)}, f32[8,128,4,128]{3,2,1,0:T(4,128)}, u32[]{:S(2)}) copy-start(f32[8,128,4,128]{3,2,1,0:T(4,128)} %broadcast_multiply_fusion) | copy-start | bytes 6291460
  328.7 286.0 %reduce-scatter.2.cloned.1.call-start = ((), (), s32[]{:S(2)}) async-start(), calls=%async_computation.4 | async-start | bytes 10485760 | tf_op jit(solution)/shard_map/reduce_scatter | solution.py:55
  330.6 106.0 %copy-start.2 = (f32[1024,512,1,1]{1,0,2,3:T(8,128)S(1)}, f32[1024,512,1,1]{1,0,2,3:T(8,128)}, u32[]{:S(2)}) copy-start(f32[1024,512,1,1]{1,0,2,3:T(8,128)} %reshape.37) | copy-start | bytes 6291460
Sparse Core Ops, SparseCore 0:
  11.1 152.3 all-gather.3
  165.4 91.1 all-gather.5
  328.8 89.7 all-gather.7
  470.0 144.6 reduce-scatter.1
where the time goes:
time: 627 us
  waiting for transfers between devices  468 us (75%)
  matrix products  83.9 us (13%)
  local copies, waits for them, and re-layouts  54.7 us (9%)
  between operations  13.2 us (2%)
  other arithmetic  6.82 us (1%)
    all_gather x1, waiting for transfers between devices, local(): panel_all = lax.all_gather(masked, 'row', axis=1, tiled=True)  152 us
    reduce_scatter x1, waiting for transfers between devices, local(): summed = lax.psum_scatter(term, 'row', scatter_dimension=0, tiled=True)  145 us
    all_gather x1, waiting for transfers between devices, local(): lax.all_gather(product_blocks, 'col', axis=3, tiled=True)  88 us
    all_gather x1, waiting for transfers between devices, local(): segment = lax.all_gather(ancestor_pivot, 'col', axis=3, tiled=True)  82.6 us
    dot_general x1, matrix products, local(): jnp.einsum('kcl,cln->kn', weights, panel_split, precision=lax.Precision.H...  54.8 us
    dot_general x1, matrix products, column_term(): jnp.einsum('kcl,kn->cln', shaped, stationary, precision=lax.Precision.HIG...  29.1 us
    reshape x1, local copies, waits for them, and re-layouts, column_term(): shaped = piece.reshape(local_rows, piece.shape[2], piece.shape[3])  18 us
    all_gather x1, local copies, waits for them, and re-layouts, local(): segment = lax.all_gather(ancestor_pivot, 'col', axis=3, tiled=True)  15.3 us
  transfers between devices with their start and end apart: 4, of which 4 were waited for; matrix products, arithmetic and copies ran while one was open for 2% of the time, Pallas kernels for 0%

commit v1 on v0

--- a/solution.py
+++ b/solution.py
@@ -2,6 +2,23 @@
 import jax.numpy as jnp
 from jax import lax
 from jax.sharding import PartitionSpec as P
+
+
+def _wait_area(inner_x):
+    which_axis = "row"
+    axis_len = lax.axis_size(which_axis)
+    rack = list(map(lambda q: (q, (q + 1) % axis_len), range(axis_len)))
+
+    def works_test(taken_in):
+        if len(taken_in) == axis_len:
+            return taken_in
+        return works_test([lax.ppermute(taken_in[0], perm=rack, axis_name=which_axis), *taken_in])
+
+    return jnp.roll(
+        jnp.concatenate(works_test([inner_x]), axis=1),
+        shift=(lax.axis_index(which_axis) + 1) * inner_x.shape[1],
+        axis=1,
+    )
 
 
 def column_term(stationary, local_rows, piece):
@@ -32,7 +49,7 @@
     local_mask = lax.dynamic_index_in_dim(local_mask, col_index, 2, keepdims=False)
     masked = child_panel * local_mask.astype(jnp.float32)[:, None, :, None]
     masked_flat = masked.reshape(local_rows, local_cols)
-    panel_all = lax.all_gather(masked, "row", axis=1, tiled=True)
+    panel_all = _wait_area(masked)
     panel_split = panel_all.reshape(anc_col_blocks, col_count * block_size, local_cols)
     segment = lax.all_gather(ancestor_pivot, "col", axis=3, tiled=True)
     length = segment.shape[3]

time: 627 us -> 567 us (0.904)
  waiting for transfers between devices: 468 us -> 376 us
  local copies, waits for them, and re-layouts: 54.7 us -> 80.8 us
    all_gather x1 -> x0, waiting for transfers between devices: 152 us -> none  [local(): panel_all = lax.all_gather(masked, 'row', axis=1, tiled=True)]
    ppermute x0 -> x3, waiting for transfers between devices: none -> 144 us  [works_test(): lax.ppermute(taken_in[0], perm=rack, axis_name=which_axis)]
    all_gather x1, waiting for transfers between devices: 82.6 us -> 0.01 us  [local(): segment = lax.all_gather(ancestor_pivot, 'col', axis=3, tiled=True)]
    unnamed x8 -> x22, local copies, waits for them, and re-layouts: 1.91 us -> 20.9 us
    dynamic_slice x0 -> x1, local copies, waits for them, and re-layouts: none -> 7.21 us  [_wait_area(): jnp.roll(jnp.concatenate(works_test([inner_x]), axis=1), shift=(lax.axis_...]
  transfers between devices with their start and end apart: 4 -> 6, of which waited for: 4 -> 5; matrix products, arithmetic and copies ran while one was open for 2% -> 8% of each run, Pallas kernels for 0% -> 0%
where the time goes in v1:
time: 567 us; the launch traced here: 566 us
  waiting for transfers between devices  376 us (66%)
  matrix products  83.9 us (15%)
  local copies, waits for them, and re-layouts  80.8 us (14%)
  between operations  13.2 us (2%)
  other arithmetic  9.15 us (2%)
    reduce_scatter x1, waiting for transfers between devices, local(): summed = lax.psum_scatter(term, 'row', scatter_dimension=0, tiled=True)  145 us
    ppermute x3, waiting for transfers between devices, works_test(): lax.ppermute(taken_in[0], perm=rack, axis_name=which_axis)  144 us
    all_gather x1, waiting for transfers between devices, local(): lax.all_gather(product_blocks, 'col', axis=3, tiled=True)  85.7 us
    dot_general x1, matrix products, local(): jnp.einsum('kcl,cln->kn', weights, panel_split, precision=lax.Precision.H...  54.8 us
    dot_general x1, matrix products, column_term(): jnp.einsum('kcl,kn->cln', shaped, stationary, precision=lax.Precision.HIG...  29.1 us
    unnamed x22, local copies, waits for them, and re-layouts  20.9 us
    reshape x1, local copies, waits for them, and re-layouts, column_term(): shaped = piece.reshape(local_rows, piece.shape[2], piece.shape[3])  18 us
    all_gather x1, local copies, waits for them, and re-layouts, local(): segment = lax.all_gather(ancestor_pivot, 'col', axis=3, tiled=True)  15.3 us
  transfers between devices with their start and end apart: 6, of which 5 were waited for; matrix products, arithmetic and copies ran while one was open for 8% of the time, Pallas kernels for 0%

profile of v1, /device:TPU:0, one launch (start us, length us, event | category | flops | bytes accessed | tf_op | source)
XLA Modules:
  0.0 565.9 jit_solution(16264722511990331249)
XLA Ops:
  6.5 0.0 all-gather.3.cloned.1.call-start
  6.5 0.7 all-gather.3.cloned.1.call-update
  7.3 0.0 all-gather.5.cloned.1.call-start
  7.3 0.8 reshape.28
  8.1 0.1 constant_dynamic-slice_fusion.1
  8.2 0.1 copy.15
  8.3 0.1 copy.9
  8.4 0.0 copy-start
  8.4 2.2 broadcast_multiply_fusion
  10.6 0.0 copy-start.1
  10.7 1.4 copy-done.1
  12.0 3.1 collective-permute-start
  15.1 47.7 %collective-permute-done = f32[8,128,4,128]{3,2,1,0:T(4,128)S(1)} collective-permute-done((f32[8,128,4,128]{3,2,1,0:T(4,128)S(1)}, f32[8,128,4,128]{3,2,1,0:T(4,128)S(1)}, u32[]{:S(2)}, u32[]{:S(2)}) %collective-permute-start) | collective-permute-done | bytes 2097184 | tf_op jit(solution)/shard_map/ppermute | solution.py:15
  62.7 0.0 copy-start.4
  62.7 1.3 copy-done.4
  64.0 0.0 collective-permute-start.1
  64.0 48.7 %collective-permute-done.1 = f32[8,128,4,128]{3,2,1,0:T(4,128)} collective-permute-done((f32[8,128,4,128]{3,2,1,0:T(4,128)S(1)}, f32[8,128,4,128]{3,2,1,0:T(4,128)}, u32[]{:S(2)}, u32[]{:S(2)}) %collective-permute-start.1) | collective-permute-done | bytes 2097184 | tf_op jit(solution)/shard_map/ppermute | solution.py:15
  112.7 0.0 collective-permute-start.2
  112.7 0.0 copy-start.5
  112.7 48.0 %collective-permute-done.2 = f32[8,128,4,128]{3,2,1,0:T(4,128)} collective-permute-done((f32[8,128,4,128]{3,2,1,0:T(4,128)}, f32[8,128,4,128]{3,2,1,0:T(4,128)}, u32[]{:S(2)}, u32[]{:S(2)}) %collective-permute-start.2) | collective-permute-done | bytes 2097184 | tf_op jit(solution)/shard_map/ppermute | solution.py:15
  160.8 3.3 constant_dynamic-update-slice_fusion.7
  164.1 3.3 constant_dynamic-update-slice_fusion.6
  167.4 0.0 copy-done.5
  167.4 1.6 constant_dynamic-update-slice_fusion.5
  169.0 0.0 copy-done
  169.0 1.7 constant_dynamic-update-slice_fusion.4
  170.7 3.2 constant_dynamic-update-slice_fusion.3
  174.0 3.2 constant_dynamic-update-slice_fusion.2
  177.2 1.7 constant_dynamic-update-slice_fusion.1
  178.9 1.7 constant_dynamic-update-slice_fusion
  180.6 7.2 %constant_dynamic-slice_fusion = f32[8,512,4,128]{3,2,1,0:T(4,128)} fusion(f32[8,1024,4,128]{3,2,1,0:T(4,128)} %constant_dynamic-update-slice_fusion, s32[]{:T(128)S(6)} %select_n.30), kind=kLoop, calls=%fused_computation.13 | loop fusion | bytes 16777220 | tf_op jit(solution)/shard_map/jit(_roll_dynamic)/dynamic_slice | solution.py:17
  187.8 10.3 %reshape.29 = f32[4,1024,512]{2,1,0:T(8,128)} reshape(f32[8,512,4,128]{3,2,1,0:T(4,128)} %constant_dynamic-slice_fusion) | data formatting | bytes 16777216 | tf_op jit(solution)/shard_map/reshape | solution.py:53
  198.2 0.0 all-gather.3.cloned.1.call-done
  198.2 0.0 copy-start.3
  198.2 15.3 %copy.10 = f32[8,128,4,1024]{3,1,0,2:T(8,128)S(1)} copy(f32[8,128,4,1024]{3,2,1,0:T(4,128)} %all-gather.3.cloned.1.call-done) | data formatting | bytes 33554432 | tf_op jit(solution)/shard_map/all_gather | solution.py:54
  213.5 0.0 copy-done.3
  213.5 0.0 copy-start.2
  213.5 54.8 %convolution_bitcast_fusion.1 = f32[64,8,8,128]{3,1,2,0:T(8,128)S(1)} fusion(f32[4,1024,512]{2,1,0:T(8,128)S(1)} %copy-done.3, f32[1024,4,1024]{2,0,1:T(8,128)S(1)} %bitcast.29), kind=kOutput, calls=%fused_computation.2 | convolution fusion | flops 25769803776 | bytes 27262976 | tf_op jit(solution)/shard_map/kcl,cln->kn/dot_general | solution.py:57
  268.4 1.8 copy.16
  270.2 0.0 all-gather.5.cloned.1.call-update
  270.2 0.0 reduce-scatter.2.cloned.1.call-start
  270.2 0.0 copy-done.2
  270.3 1.9 reshape.37
  272.1 0.0 copy-start.6
  272.1 85.7 %all-gather.5.cloned.1.call-done = f32[8,128,4,1024]{1,0,3,2:T(8,128)} async-done(((f32[8,128,4,128]{1,0,3,2:T(8,128)}), f32[8,128,4,1024]{1,0,3,2:T(8,128)}) %all-gather.5.cloned.1.call-update) | async-done | bytes 16777232 | tf_op jit(solution)/shard_map/all_gather | solution.py:66
  357.8 18.0 %reshape.32 = f32[1024,4,1024]{0,2,1:T(8,128)} reshape(f32[8,128,4,1024]{1,0,3,2:T(8,128)} %all-gather.5.cloned.1.call-done) | data formatting | bytes 33554432 | tf_op jit(solution)/shard_map/reshape | solution.py:25
  375.8 0.0 copy-done.6
  375.8 29.1 %convolution_bitcast_fusion = f32[4,8,128,512]{3,2,0,1:T(8,128)S(1)} fusion(f32[8,4,128,1024]{3,2,1,0:T(8,128)} %bitcast.30, f32[1024,512,1,1]{1,0,2,3:T(8,128)S(1)} %copy-done.6), kind=kOutput, calls=%fused_computation | convolution fusion | flops 25769803776 | bytes 27262976 | tf_op jit(solution)/shard_map/kcl,kn->cln/dot_general | solution.py:26
  404.9 4.2 copy.12
  409.1 0.0 reduce-scatter.2.cloned.1.call-update
  409.2 144.8 %reduce-scatter.2.cloned.1.call-done = f32[1024,512]{1,0:T(8,128)} async-done(((f32[4096,512]{1,0:T(8,128)}), f32[1024,512]{1,0:T(8,128)}) %reduce-scatter.2.cloned.1.call-update) | async-done | bytes 2097168 | tf_op jit(solution)/shard_map/reduce_scatter | solution.py:72
  553.9 1.9 reshape.35
  555.9 3.5 add.35
  (1 shorter events, 0.0 us)
Async XLA Ops:
  6.5 191.6 %all-gather.3.cloned.1.call-start = ((), (), s32[]{:S(2)}) async-start(), calls=%async_computation.1 | async-start | bytes 18874368 | tf_op jit(solution)/shard_map/all_gather | solution.py:54
  7.3 350.6 %all-gather.5.cloned.1.call-start = ((), (), s32[]{:S(2)}) async-start(), calls=%async_computation.2 | async-start | bytes 18874368 | tf_op jit(solution)/shard_map/all_gather | solution.py:66
  8.4 160.6 %copy-start = (f32[8,128,4,128]{3,2,1,0:T(4,128)S(1)}, f32[8,128,4,128]{3,2,1,0:T(4,128)}, u32[]{:S(2)}) copy-start(f32[8,128,4,128]{3,2,1,0:T(4,128)} %param.6) | copy-start | bytes 6291460
  10.6 1.4 copy-start.1
  12.0 50.7 %collective-permute-start = (f32[8,128,4,128]{3,2,1,0:T(4,128)S(1)}, f32[8,128,4,128]{3,2,1,0:T(4,128)S(1)}, u32[]{:S(2)}, u32[]{:S(2)}) collective-permute-start(f32[8,128,4,128]{3,2,1,0:T(4,128)S(1)} %broadcast_multiply_fusion), channel_id=1, source_target_pairs={{0,8},{8,16},{16,24},{24,0},{1,9},{9,17},{17,25},{25,1},{2,10},{10... | collective-permute-start | bytes 6291464 | tf_op jit(solution)/shard_map/ppermute | solution.py:15
  62.7 1.3 copy-start.4
  64.0 48.7 %collective-permute-start.1 = (f32[8,128,4,128]{3,2,1,0:T(4,128)S(1)}, f32[8,128,4,128]{3,2,1,0:T(4,128)}, u32[]{:S(2)}, u32[]{:S(2)}) collective-permute-start(f32[8,128,4,128]{3,2,1,0:T(4,128)S(1)} %collective-permute-done), channel_id=1, source_target_pairs={{0,8},{8,16},{16,24},{24,0},{1,9},{9,17},{17,25},{25,1},{2,10},{10... | collective-permute-start | bytes 6291464 | tf_op jit(solution)/shard_map/ppermute | solution.py:15
  112.7 48.1 %collective-permute-start.2 = (f32[8,128,4,128]{3,2,1,0:T(4,128)}, f32[8,128,4,128]{3,2,1,0:T(4,128)}, u32[]{:S(2)}, u32[]{:S(2)}) collective-permute-start(f32[8,128,4,128]{3,2,1,0:T(4,128)} %collective-permute-done.1), channel_id=1, source_target_pairs={{0,8},{8,16},{16,24},{24,0},{1,9},{9,17},{17,25},{25,1},{2,10},{10... | collective-permute-start | bytes 6291464 | tf_op jit(solution)/shard_map/ppermute | solution.py:15
  112.7 54.6 %copy-start.5 = (f32[8,128,4,128]{3,2,1,0:T(4,128)S(1)}, f32[8,128,4,128]{3,2,1,0:T(4,128)}, u32[]{:S(2)}) copy-start(f32[8,128,4,128]{3,2,1,0:T(4,128)} %copy-done.4) | copy-start | bytes 6291460
  198.2 15.4 %copy-start.3 = (f32[4,1024,512]{2,1,0:T(8,128)S(1)}, f32[4,1024,512]{2,1,0:T(8,128)}, u32[]{:S(2)}) copy-start(f32[4,1024,512]{2,1,0:T(8,128)} %reshape.29) | copy-start | bytes 25165828
  213.5 56.7 %copy-start.2 = (f32[8,128,4,128]{3,2,1,0:T(4,128)S(1)}, f32[8,128,4,128]{3,2,1,0:T(4,128)}, u32[]{:S(2)}) copy-start(f32[8,128,4,128]{3,2,1,0:T(4,128)} %copy-done.1) | copy-start | bytes 6291460
  270.2 283.8 %reduce-scatter.2.cloned.1.call-start = ((), (), s32[]{:S(2)}) async-start(), calls=%async_computation.3 | async-start | bytes 10485760 | tf_op jit(solution)/shard_map/reduce_scatter | solution.py:72
  272.1 103.7 %copy-start.6 = (f32[1024,512,1,1]{1,0,2,3:T(8,128)S(1)}, f32[1024,512,1,1]{1,0,2,3:T(8,128)}, u32[]{:S(2)}) copy-start(f32[1024,512,1,1]{1,0,2,3:T(8,128)} %reshape.37) | copy-start | bytes 6291460
Sparse Core Ops, SparseCore 0:
  9.2 95.7 all-gather.2
  270.3 87.4 all-gather.4
  409.3 144.6 reduce-scatter.1
